TPU v7x, 256 devices: a whole 4x4x8 slice. The times are simulated.
256 devices in a mesh: row: 128 (over y, z, x), head: 2 (over core).
Axes of the slice: x: 4, y: 4, z: 8, core: 2. Of those that a mesh axis runs over, the one named last changes fastest.
Arguments:
- query_single: bfloat16 [128, 384], P('row'), may hold values from -6 to 6
- key_single: bfloat16 [8192, 384], P('row'), may hold values from -6 to 6
- pair: bfloat16 [128, 8192, 128], P('row'), may hold values from -6 to 32
- query_frames: float32 [12, 128], P(None, 'row'), may hold values from -2.5 to 2.5, as said below
- key_frames: float32 [12, 8192], P(None, 'row'), may hold values from -2.5 to 2.5, as said below
- w_query: bfloat16 [384, 96], P(None, 'head'), may hold values from -0.3125 to 0.3125
- w_key: bfloat16 [384, 96], P(None, 'head'), may hold values from -0.3125 to 0.3125
- w_value: bfloat16 [384, 96], P(None, 'head'), may hold values from -0.3125 to 0.3125
- w_query_points: bfloat16 [384, 72], P(None, 'head'), may hold values from -0.3125 to 0.3125
- w_key_points: bfloat16 [384, 72], P(None, 'head'), may hold values from -0.3125 to 0.3125
- w_value_points: bfloat16 [384, 144], P(None, 'head'), may hold values from -0.3125 to 0.3125
- head_weight: float32 [6], P('head'), may hold values from -2.5 to 0.5
- bias_weight: bfloat16 [6, 128], P('head'), as said below
- w_out: bfloat16 [1056, 384], P('head'), may hold values from -0.1875 to 0.1875
- d_out: bfloat16 [128, 384], P('row'), may hold values from -24 to 24
Outputs:
- output: bfloat16 [128, 384], P('row')
- grad_query: float32 [128, 384], P('row')
- grad_keys: float32 [8192, 384], P('row')
Inputs may be any that keep to these rules, and one draw needn't show every extreme that they name: `bias_weight`: entries within -2.5 and 2.5 over the square root of 128. `query_frames`: rows 0 to 8 of each column form a rotation matrix. `key_frames`: rows 0 to 8 of each column form a rotation matrix.
All inputs are finite; a program needn't handle non-finite values.
Results may differ from a plain program's by a relative error of at most 0.012.
The roundings to bfloat16 on the way count: a program that leaves them out, or rounds other values in their place, can miss the bound.
Values may be sent and summed in bfloat16 or wider, within the bound.
A program may use at most 64 MiB of HBM per device.

v0:
```python
import math
import jax
import jax.numpy as jnp
from jax import lax
from jax.sharding import PartitionSpec as P

C = 16
PQ = 4
PV = 8
LOGIT_SCALE = math.sqrt(1.0 / 3.0)


def point_scale(points):
    return math.sqrt(2.0 / (9.0 * points))


def product(form, former, latter):
    return jnp.einsum(form, former, latter, preferred_element_type=jnp.float32)


def frame_parts(frames):
    columns = frames.shape[1]
    return (frames[:9].reshape(3, 3, columns), frames[9:12])


def rotate(vectors, rotation):
    return jnp.einsum("xyn,nhpy->nhpx", rotation, vectors, precision=lax.Precision.HIGHEST)


def unrotate(vectors, rotation):
    return jnp.einsum("xyn,nhpx->nhpy", rotation, vectors, precision=lax.Precision.HIGHEST)


def split_columns(packed, extents, axis_index):
    pieces = []
    cursor = 0
    for extent in extents:
        pieces.append(lax.slice_in_dim(packed, cursor, cursor + extent, axis=axis_index))
        cursor = cursor + extent
    return pieces


def key_side(key_single, key_frames, w_key, w_value, w_key_points, w_value_points, head_count):
    rows_k = key_single.shape[0]
    rotation, offset = frame_parts(key_frames)
    offset_rows = jnp.transpose(offset)[:, None, None, :]
    keys_b = jnp.dot(key_single, w_key, preferred_element_type=jnp.float32).astype(jnp.bfloat16)
    values_b = jnp.dot(key_single, w_value, preferred_element_type=jnp.float32).astype(jnp.bfloat16)
    local_k = jnp.dot(key_single, w_key_points, preferred_element_type=jnp.float32).reshape(
        rows_k, head_count, PQ, 3
    )
    key_pts = (rotate(local_k, rotation) + offset_rows).astype(jnp.bfloat16).reshape(rows_k, -1)
    local_v = jnp.dot(key_single, w_value_points, preferred_element_type=jnp.float32).reshape(
        rows_k, head_count, PV, 3
    )
    value_pts = (rotate(local_v, rotation) + offset_rows).astype(jnp.bfloat16).reshape(rows_k, -1)
    return (keys_b, values_b, key_pts, value_pts)


def query_pass(
    query_single,
    pair,
    query_frames,
    w_query,
    w_query_points,
    head_weight,
    bias_weight,
    w_out,
    d_out,
    keys_all,
    values_all,
    kp_all,
    vp_all,
):
    rows_q = query_single.shape[0]
    head_count = head_weight.shape[0]
    rotation, offset = frame_parts(query_frames)
    offset_rows = jnp.transpose(offset)[:, None, None, :]
    point_gain = (jax.nn.softplus(head_weight) * point_scale(PQ))[None, :, None]
    query_b = (
        jnp.dot(query_single, w_query, preferred_element_type=jnp.float32)
        .astype(jnp.bfloat16)
        .reshape(rows_q, head_count, C)
    )
    local_q = jnp.dot(query_single, w_query_points, preferred_element_type=jnp.float32).reshape(
        rows_q, head_count, PQ, 3
    )
    query_pts = (
        (rotate(local_q, rotation) + offset_rows)
        .astype(jnp.bfloat16)
        .reshape(rows_q, head_count, 3 * PQ)
    )
    query_sq = jnp.sum(jnp.square(query_pts.astype(jnp.float32)), axis=-1)
    key_sq = jnp.sum(jnp.square(kp_all.astype(jnp.float32)), axis=-1)
    pair_bias = product("hc,qkc->qhk", bias_weight, pair)
    distance = (
        query_sq[:, :, None]
        + jnp.transpose(key_sq)[None, :, :]
        - 2.0 * product("qhe,khe->qhk", query_pts, kp_all)
    )
    logits = LOGIT_SCALE * (
        product("qhc,khc->qhk", query_b, keys_all) / math.sqrt(C)
        + pair_bias
        - 0.5 * point_gain * distance
    )
    attention = jax.nn.softmax(logits, axis=-1)
    attention_b = attention.astype(jnp.bfloat16)
    attended = product("qhk,khc->qhc", attention_b, values_all)
    point_sum = product("qhk,khe->qhe", attention_b, vp_all).reshape(rows_q, head_count, PV, 3)
    pair_out = product("qhk,qkc->qhc", attention_b, pair)
    local_pts = unrotate(point_sum - offset_rows, rotation)
    lengths = jnp.sqrt(1.0 + jnp.sum(jnp.square(local_pts), axis=-1))
    features = jnp.concatenate(
        [attended, local_pts.reshape(rows_q, head_count, 3 * PV), lengths, pair_out], axis=-1
    )
    features = features.astype(jnp.bfloat16).reshape(rows_q, -1)
    output_part = jnp.dot(features, w_out, preferred_element_type=jnp.float32)
    d_features = jnp.dot(d_out, jnp.transpose(w_out), preferred_element_type=jnp.float32).reshape(
        rows_q, head_count, -1
    )
    d_attended = d_features[:, :, :C].astype(jnp.bfloat16)
    d_local = d_features[:, :, C : C + 3 * PV].reshape(rows_q, head_count, PV, 3)
    d_lengths = d_features[:, :, C + 3 * PV : C + 4 * PV]
    d_pair = d_features[:, :, C + 4 * PV :].astype(jnp.bfloat16)
    d_local = d_local + (d_lengths / lengths)[..., None] * local_pts
    d_points = rotate(d_local, rotation).astype(jnp.bfloat16).reshape(rows_q, head_count, 3 * PV)
    d_attention = (
        product("qhc,khc->qhk", d_attended, values_all)
        + product("qhe,khe->qhk", d_points, vp_all)
        + product("qhc,qkc->qhk", d_pair, pair)
    )
    row_total = jnp.sum(attention * d_attention, axis=-1, keepdims=True)
    score_b = (LOGIT_SCALE * attention * (d_attention - row_total)).astype(jnp.bfloat16)
    d_query = product("qhk,khc->qhc", score_b, keys_all) / math.sqrt(C)
    score_rows = jnp.sum(score_b.astype(jnp.float32), axis=-1)[:, :, None]
    d_qpts = point_gain * (
        product("qhk,khe->qhe", score_b, kp_all) - score_rows * query_pts.astype(jnp.float32)
    )
    d_qlocal = (
        unrotate(d_qpts.reshape(rows_q, head_count, PQ, 3), rotation)
        .astype(jnp.bfloat16)
        .reshape(rows_q, -1)
    )
    grad_part = jnp.dot(
        d_query.astype(jnp.bfloat16).reshape(rows_q, -1),
        jnp.transpose(w_query),
        preferred_element_type=jnp.float32,
    )
    grad_part = grad_part + jnp.dot(
        d_qlocal, jnp.transpose(w_query_points), preferred_element_type=jnp.float32
    )
    query_side = jnp.concatenate(
        [
            query_b.reshape(rows_q, -1),
            query_pts.reshape(rows_q, -1),
            d_attended.reshape(rows_q, -1),
            d_points.reshape(rows_q, -1),
        ],
        axis=1,
    )
    return (output_part, grad_part, query_side, attention_b, score_b)


def key_terms(attention_b, score_b, query_side, key_points, point_gain, head_count):
    count_q = query_side.shape[0]
    count_k = key_points.shape[0]
    side_parts = split_columns(
        query_side, [head_count * C, head_count * 3 * PQ, head_count * C, head_count * 3 * PV], 1
    )
    query_b = side_parts[0].reshape(count_q, head_count, C)
    query_pts = side_parts[1].reshape(count_q, head_count, 3 * PQ)
    grad_att = side_parts[2].reshape(count_q, head_count, C)
    grad_pts = side_parts[3].reshape(count_q, head_count, 3 * PV)
    d_key = product("qhk,qhc->khc", score_b, query_b) / math.sqrt(C)
    score_sum = jnp.sum(score_b.astype(jnp.float32), axis=0)
    d_kpts = point_gain * (
        product("qhk,qhe->khe", score_b, query_pts)
        - jnp.transpose(score_sum)[:, :, None] * key_points.astype(jnp.float32)
    )
    d_value = product("qhk,qhc->khc", attention_b, grad_att)
    d_vpts = product("qhk,qhe->khe", attention_b, grad_pts)
    return jnp.concatenate(
        [
            d_key.reshape(count_k, -1),
            d_value.reshape(count_k, -1),
            d_kpts.reshape(count_k, -1),
            d_vpts.reshape(count_k, -1),
        ],
        axis=1,
    )


def key_finish(key_rows, key_frames, w_key, w_value, w_key_points, w_value_points, head_count):
    rows_k = key_rows.shape[0]
    rotation, offset = frame_parts(key_frames)
    pieces = split_columns(
        key_rows, [head_count * C, head_count * C, head_count * 3 * PQ, head_count * 3 * PV], 1
    )
    kp_local = (
        unrotate(pieces[2].reshape(rows_k, head_count, PQ, 3), rotation)
        .astype(jnp.bfloat16)
        .reshape(rows_k, -1)
    )
    vp_local = (
        unrotate(pieces[3].reshape(rows_k, head_count, PV, 3), rotation)
        .astype(jnp.bfloat16)
        .reshape(rows_k, -1)
    )
    result = jnp.dot(
        pieces[0].astype(jnp.bfloat16), jnp.transpose(w_key), preferred_element_type=jnp.float32
    )
    result = result + jnp.dot(
        pieces[1].astype(jnp.bfloat16), jnp.transpose(w_value), preferred_element_type=jnp.float32
    )
    result = result + jnp.dot(
        kp_local, jnp.transpose(w_key_points), preferred_element_type=jnp.float32
    )
    return result + jnp.dot(
        vp_local, jnp.transpose(w_value_points), preferred_element_type=jnp.float32
    )


def shards(
    query_single,
    key_single,
    pair,
    query_frames,
    key_frames,
    w_query,
    w_key,
    w_value,
    w_query_points,
    w_key_points,
    w_value_points,
    head_weight,
    bias_weight,
    w_out,
    d_out,
):
    head_count = head_weight.shape[0]
    keys_b, values_b, key_pts, value_pts = key_side(
        key_single, key_frames, w_key, w_value, w_key_points, w_value_points, head_count
    )
    packed = jnp.concatenate([keys_b, values_b, key_pts, value_pts], axis=1)
    gathered = lax.all_gather(packed, "row", axis=0, tiled=True)
    total_keys = gathered.shape[0]
    pieces = split_columns(
        gathered, [head_count * C, head_count * C, head_count * 3 * PQ, head_count * 3 * PV], 1
    )
    keys_all = pieces[0].reshape(total_keys, head_count, C)
    values_all = pieces[1].reshape(total_keys, head_count, C)
    kp_all = pieces[2].reshape(total_keys, head_count, 3 * PQ)
    vp_all = pieces[3].reshape(total_keys, head_count, 3 * PV)
    output_part, grad_part, query_side, attention_b, score_b = query_pass(
        query_single,
        pair,
        query_frames,
        w_query,
        w_query_points,
        head_weight,
        bias_weight,
        w_out,
        d_out,
        keys_all,
        values_all,
        kp_all,
        vp_all,
    )
    output = lax.psum(output_part, "head").astype(jnp.bfloat16)
    point_gain = (jax.nn.softplus(head_weight) * point_scale(PQ))[None, :, None]
    scores = jnp.concatenate([attention_b, score_b], axis=1)
    rows_n = lax.axis_size("row")
    local_k = key_single.shape[0]
    scores = scores.reshape(2 * head_count, rows_n, local_k)
    scores = lax.all_to_all(scores, "row", split_axis=1, concat_axis=1, tiled=True)
    scores = jnp.transpose(scores, (1, 0, 2))
    side_all = lax.all_gather(query_side, "row", axis=0, tiled=True)
    key_rows = key_terms(
        scores[:, :head_count],
        scores[:, head_count:],
        side_all,
        key_pts.reshape(local_k, head_count, 3 * PQ),
        point_gain,
        head_count,
    )
    grad_keys_part = key_finish(
        key_rows, key_frames, w_key, w_value, w_key_points, w_value_points, head_count
    )
    grad_query, grad_keys = lax.psum((grad_part, grad_keys_part), "head")
    return (output, grad_query, grad_keys)


def solution(mesh):
    return jax.shard_map(
        shards,
        mesh=mesh,
        in_specs=(
            P("row", None),
            P("row", None),
            P("row", None, None),
            P(None, "row"),
            P(None, "row"),
            P(None, "head"),
            P(None, "head"),
            P(None, "head"),
            P(None, "head"),
            P(None, "head"),
            P(None, "head"),
            P("head"),
            P("head", None),
            P("head", None),
            P("row", None),
        ),
        out_specs=(P("row", None), P("row", None), P("row", None)),
        check_vma=False,
    )
```

profile of v0, /device:TPU:1, one launch (start us, length us, event | category | flops | bytes accessed | tf_op | source)
XLA Modules:
  0.0 621.8 jit_solution(9938110551300458424)
XLA Ops:
  7.2 0.8 slice_bitcast_fusion
  8.1 0.7 reshape.324
  8.9 0.9 fusion.64
  10.2 7.5 %fusion.65 = f32[64,3,4,3]{2,3,1,0:T(4,128)S(1)} fusion(f32[64,3,4,3]{3,2,1,0:T(4,128)S(1)} %copy.139, f32[3,3,64,1]{0,1,3,2:T(4,128)S(1)} %copy.198), kind=kOutput, calls=%fused_computation.113 | convolution fusion | flops 82944 | bytes 20736 | tf_op jit(solution)/shard_map/xyn,nhpy->nhpx/dot_general | solution.py:27
  18.4 1.1 fusion.7
  19.7 0.9 convolution_convert_fusion.3
  20.6 0.9 convolution_convert_fusion.4
  21.5 0.7 copy.148
  22.7 0.8 reshape.333
  24.4 0.7 reshape_reshape.13
  25.1 0.6 copy.166
  25.7 0.7 reshape.336
  26.3 0.9 fusion.18
  27.3 0.6 sub.56
  27.9 0.7 reshape.334
  28.8 0.7 copy.157
  29.5 0.6 fusion.62
  30.0 0.7 reshape.349
  30.7 0.5 broadcast_multiply_fusion
  31.2 108.1 %all-gather.3.cloned.1.call-done = bf16[8192,204]{1,0:T(8,128)(2,1)} async-done(((bf16[64,204]{1,0:T(8,128)(2,1)}), bf16[8192,204]{1,0:T(8,128)(2,1)}) %all-gather.3.cloned.1.call-update) | async-done | bytes 3342352 | tf_op jit(solution)/shard_map/all_gather | solution.py:245
  139.3 4.2 slice.77
  143.5 2.9 copy.151
  146.5 1.2 reshape.335
  147.7 1.0 multiply_reduce_fusion
  149.0 4.9 fusion.59
  153.8 2.7 copy.211
  156.5 1.4 fusion.67
  157.9 1.7 fusion.63
  159.9 0.7 fusion.57
  160.6 3.6 slice.78
  164.2 3.8 copy.212
  167.9 1.7 fusion.29
  169.7 0.7 bitcast_subtract_fusion.1
  170.3 0.7 sub.59
  171.0 1.6 fusion.61
  172.6 0.7 fusion.41
  173.4 1.4 convolution_convert_fusion.6
  174.8 1.4 copy.158
  176.2 1.3 reshape.404
  177.5 1.3 reshape_reshape.14
  178.8 0.8 maximum_bitcast_fusion
  179.6 304.1 %all-gather = bf16[128,1,204]{2,1,0:T(2,128)(2,1)} all-gather(bf16[1,1,204]{2,1,0:T(2,128)(2,1)S(1)} %maximum_bitcast_fusion), channel_id=1, replica_groups=mesh['row'=128,'head'=2] {'row'}, dimensions={0}, use_global_device_ids=true | all-gather | bytes 52632 | tf_op jit(solution)/shard_map/all_gather | solution.py:277
  483.6 1.6 copy.163
  485.3 1.3 slice.88
  486.6 1.3 slice.87
  487.9 2.2 fusion.70
  490.1 2.6 copy.210
  492.8 1.4 fusion.50
  494.2 1.8 fusion.20
  496.0 0.8 convert_reduce_fusion
  496.8 1.0 fusion.25
  498.2 0.4 fusion.31
  498.7 0.4 fusion.15
  499.4 0.9 reshape.419
  500.3 6.1 all-to-all-start
  508.2 0.8 fusion.60
  509.0 8.4 %all-to-all-done = bf16[128,2,192]{2,1,0:T(2,128)(2,1)S(1)} async-done(((bf16[128,2,192]{2,1,0:T(2,128)(2,1)}), bf16[128,2,192]{2,1,0:T(2,128)(2,1)S(1)}, u32[]{:S(2)}, u32[]{:S(2)}) %all-to-all-start) | async-done | bytes 98336 | tf_op jit(solution)/shard_map/all_to_all | solution.py:275
  517.8 0.9 convolution_bitcast_fusion.1
  519.0 1.0 convolution_convert_fusion
  520.6 7.4 %convolution_convert_fusion.1 = bf16[64,3,4,3]{2,3,1,0:T(4,128)(2,1)S(1)} fusion(f32[64,3,4,3]{3,2,1,0:T(4,128)S(1)} %copy.169, f32[3,3,64,1]{0,1,3,2:T(4,128)S(1)} %copy.198), kind=kOutput, calls=%fused_computation.12 | convolution fusion | flops 85248 | bytes 16128 | tf_op jit(solution)/shard_map/xyn,nhpx->nhpy/dot_general | solution.py:31
  529.1 0.8 convolution_add_fusion.2
  530.2 65.1 %all-reduce = (bf16[1,384]{1,0:T(2,128)(2,1)}, f32[1,384]{1,0:T(1,128)}) all-reduce(f32[1,384]{1,0:T(1,128)S(1)} %fusion.69, f32[1,384]{1,0:T(1,128)S(1)} %add.116), channel_id=1, replica_groups=mesh['row'=128,'head'=2] {'head'}, use_global_device_ids=true, to_apply=%region_5.6 | all-reduce | flops 768 | bytes 5376 | tf_op jit(solution)/shard_map/psum | solution.py:269
  595.2 18.1 %all-reduce.3.cloned.1.call-done = f32[64,384]{1,0:T(8,128)} async-done(((f32[64,384]{1,0:T(8,128)}), f32[64,384]{1,0:T(8,128)}) %all-reduce.3.cloned.1.call-update) | async-done | bytes 98320 | tf_op jit(solution)/shard_map/psum | solution.py:289
  613.4 1.5 copy.242
  (137 shorter events, 8.5 us)
Async XLA Ops:
  7.2 150.7 %copy-start = (bf16[1,8192,128]{2,1,0:T(8,128)(2,1)S(1)}, bf16[1,8192,128]{2,1,0:T(8,128)(2,1)}, u32[]{:S(2)}) copy-start(bf16[1,8192,128]{2,1,0:T(8,128)(2,1)} %param.17) | copy-start | bytes 6291460
  7.2 10.8 %copy-start.4 = (bf16[64,384]{1,0:T(8,128)(2,1)S(1)}, bf16[64,384]{1,0:T(8,128)(2,1)}, u32[]{:S(2)}) copy-start(bf16[64,384]{1,0:T(8,128)(2,1)} %param.16) | copy-start | bytes 147460
  7.2 10.8 %copy-start.6 = (bf16[384,72]{0,1:T(8,128)(2,1)S(1)}, bf16[384,72]{0,1:T(8,128)(2,1)}, u32[]{:S(2)}) copy-start(bf16[384,72]{0,1:T(8,128)(2,1)} %param.25) | copy-start | bytes 165892
  7.2 132.1 %all-gather.3.cloned.1.call-start = ((), (), s32[]{:S(2)}) async-start(), calls=%async_computation.1 | async-start | bytes 4227072 | tf_op jit(solution)/shard_map/all_gather | solution.py:245
  8.8 13.5 %copy-start.3 = (bf16[528,384]{1,0:T(8,128)(2,1)S(1)}, bf16[528,384]{1,0:T(8,128)(2,1)}, u32[]{:S(2)}) copy-start(bf16[528,384]{1,0:T(8,128)(2,1)} %param.28) | copy-start | bytes 1216516
  8.8 13.5 %copy-start.25 = (bf16[1,384]{1,0:T(2,128)(2,1)S(1)}, bf16[1,384]{1,0:T(2,128)(2,1)}, u32[]{:S(2)}) copy-start(bf16[1,384]{1,0:T(2,128)(2,1)} %param.29) | copy-start | bytes 2308
  9.9 12.7 %copy-start.29 = (f32[12,1]{0,1:T(1,128)S(1)}, f32[12,1]{0,1:T(1,128)}, u32[]{:S(2)}) copy-start(f32[12,1]{0,1:T(1,128)} %param.18) | copy-start | bytes 148
  10.1 13.4 %copy-start.28 = (bf16[1,384]{1,0:T(2,128)(2,1)S(1)}, bf16[1,384]{1,0:T(2,128)(2,1)}, u32[]{:S(2)}) copy-start(bf16[1,384]{1,0:T(2,128)(2,1)} %param.15) | copy-start | bytes 2308
  10.1 20.5 %copy-start.30 = (f32[3]{0:T(128)S(1)}, f32[3]{0:T(128)}, u32[]{:S(2)}) copy-start(f32[3]{0:T(128)} %param.26) | copy-start | bytes 40
  22.5 121.0 %copy-start.16 = (f32[1,3,176]{2,1,0:T(4,128)}, f32[1,3,176]{2,1,0:T(4,128)S(1)}, u32[]{:S(2)}) copy-start(f32[1,3,176]{2,1,0:T(4,128)S(1)} %copy.189) | copy-start | bytes 6340
  22.6 121.0 %copy-start.18 = (bf16[1,3,176]{2,1,0:T(4,128)(2,1)}, bf16[1,3,176]{2,1,0:T(4,128)(2,1)S(1)}, u32[]{:S(2)}) copy-start(bf16[1,3,176]{2,1,0:T(4,128)(2,1)S(1)} %copy.237) | copy-start | bytes 3172
  22.7 4.6 copy-start.19
  27.2 116.3 %copy-start.24 = (bf16[48]{0:T(256)(128)(2,1)}, bf16[48]{0:T(256)(128)(2,1)S(1)}, u32[]{:S(2)}) copy-start(bf16[48]{0:T(256)(128)(2,1)S(1)} %fusion.18) | copy-start | bytes 292
  153.8 4.1 copy-start.27
  492.8 4.0 copy-start.5
  494.2 3.6 copy-start.1
  496.0 2.2 copy-start.2
  498.6 8.1 %copy-start.13 = (bf16[128,36]{0,1:T(8,128)(2,1)S(1)}, bf16[128,36]{0,1:T(8,128)(2,1)}, u32[]{:S(2)}) copy-start(bf16[128,36]{0,1:T(8,128)(2,1)} %slice.87) | copy-start | bytes 27652
  498.6 8.1 %copy-start.20 = (bf16[3,12]{1,0:T(4,128)(2,1)S(1)}, bf16[3,12]{1,0:T(4,128)(2,1)}, u32[]{:S(2)}) copy-start(bf16[3,12]{1,0:T(4,128)(2,1)} %reshape.336) | copy-start | bytes 220
  498.6 8.1 %copy-start.21 = (f32[3]{0:T(128)S(1)}, f32[3]{0:T(128)}, u32[]{:S(2)}) copy-start(f32[3]{0:T(128)} %get-tuple-element.5) | copy-start | bytes 40
  498.6 8.1 %copy-start.23 = (f32[3]{0:T(128)S(1)}, f32[3]{0:T(128)}, u32[]{:S(2)}) copy-start(f32[3]{0:T(128)} %get-tuple-element.7) | copy-start | bytes 40
  498.6 8.1 %copy-start.26 = (f32[3,1,12]{2,1,0:T(1,128)S(1)}, f32[3,1,12]{2,1,0:T(1,128)}, u32[]{:S(2)}) copy-start(f32[3,1,12]{2,1,0:T(1,128)} %fusion.25) | copy-start | bytes 436
  498.6 8.3 %copy-start.15 = (f32[3,3]{1,0:T(4,128)S(1)}, f32[3,3]{1,0:T(4,128)}, u32[]{:S(2)}) copy-start(f32[3,3]{1,0:T(4,128)} %reshape.334) | copy-start | bytes 112
  498.6 8.9 %copy-start.14 = (bf16[384,48]{0,1:T(8,128)(2,1)S(1)}, bf16[384,48]{0,1:T(8,128)(2,1)}, u32[]{:S(2)}) copy-start(bf16[384,48]{0,1:T(8,128)(2,1)} %param.20) | copy-start | bytes 110596
  498.6 9.0 %copy-start.17 = (bf16[3,8,3]{1,2,0:T(4,128)(2,1)S(1)}, bf16[3,8,3]{1,2,0:T(4,128)(2,1)}, u32[]{:S(2)}) copy-start(bf16[3,8,3]{1,2,0:T(4,128)(2,1)} %get-tuple-element.15) | copy-start | bytes 436
  499.2 20.9 %copy-start.12 = (f32[64,3,4,3]{0,1,3,2:T(4,128)S(1)}, f32[64,3,4,3]{0,1,3,2:T(4,128)}, u32[]{:S(2)}) copy-start(f32[64,3,4,3]{0,1,3,2:T(4,128)} %copy.166) | copy-start | bytes 27652
  499.2 20.9 %copy-start.22 = (f32[3]{0:T(128)S(1)}, f32[3]{0:T(128)}, u32[]{:S(2)}) copy-start(f32[3]{0:T(128)} %get-tuple-element.5) | copy-start | bytes 40
  500.3 17.1 %all-to-all-start = ((bf16[128,2,192]{2,1,0:T(2,128)(2,1)}), bf16[128,2,192]{2,1,0:T(2,128)(2,1)S(1)}, u32[]{:S(2)}, u32[]{:S(2)}) async-start(bf16[128,2,192]{2,1,0:T(2,128)(2,1)} %reshape.419), calls=%async_computation | async-start | bytes 262144 | tf_op jit(solution)/shard_map/all_to_all | solution.py:275
  506.4 107.0 %all-reduce.3.cloned.1.call-start = ((), (), s32[]{:S(2)}) async-start(), calls=%async_computation.2 | async-start | bytes 196608 | tf_op jit(solution)/shard_map/psum | solution.py:289
  508.2 20.3 %copy-start.8 = (bf16[384,48]{0,1:T(8,128)(2,1)S(1)}, bf16[384,48]{0,1:T(8,128)(2,1)}, u32[]{:S(2)}) copy-start(bf16[384,48]{0,1:T(8,128)(2,1)} %param.21) | copy-start | bytes 110596
  509.0 19.7 %copy-start.9 = (bf16[384,48]{0,1:T(8,128)(2,1)S(1)}, bf16[384,48]{0,1:T(8,128)(2,1)}, u32[]{:S(2)}) copy-start(bf16[384,48]{0,1:T(8,128)(2,1)} %param.22) | copy-start | bytes 110596
  517.5 11.4 %copy-start.11 = (bf16[384,36]{0,1:T(8,128)(2,1)S(1)}, bf16[384,36]{0,1:T(8,128)(2,1)}, u32[]{:S(2)}) copy-start(bf16[384,36]{0,1:T(8,128)(2,1)} %param.24) | copy-start | bytes 82948
  517.5 11.6 %copy-start.7 = (bf16[384,72]{0,1:T(8,128)(2,1)S(1)}, bf16[384,72]{0,1:T(8,128)(2,1)}, u32[]{:S(2)}) copy-start(bf16[384,72]{0,1:T(8,128)(2,1)} %param.25) | copy-start | bytes 165892
  518.7 11.3 %copy-start.10 = (bf16[384,36]{0,1:T(8,128)(2,1)S(1)}, bf16[384,36]{0,1:T(8,128)(2,1)}, u32[]{:S(2)}) copy-start(bf16[384,36]{0,1:T(8,128)(2,1)} %param.23) | copy-start | bytes 82948
Sparse Core Ops, SparseCore 0:
  22.4 116.8 all-gather.2
  530.1 83.2 all-reduce.2
where the time goes:
time: 623 us; the launch traced here: 622 us
  blocking collectives  369 us (59%)
  waiting for transfers between devices  135 us (22%)
  local copies, waits for them, and re-layouts  50.5 us (8%)
  matrix products  40.5 us (7%)
  between operations  14.7 us (2%)
  starting transfers between devices  6.41 us (1%)
    all_gather x1, blocking collectives, shards(): side_all = lax.all_gather(query_side, 'row', axis=0, tiled=True)  304 us
    all_gather x1, waiting for transfers between devices, shards(): gathered = lax.all_gather(packed, 'row', axis=0, tiled=True)  108 us
    psum x1, blocking collectives, shards(): output = lax.psum(output_part, 'head').astype(jnp.bfloat16)  65.1 us
    slice x7, local copies, waits for them, and re-layouts, split_columns(): lax.slice_in_dim(packed, cursor, cursor + extent, axis=axis_index)  19 us
    psum x1, waiting for transfers between devices, shards(): grad_query, grad_keys = lax.psum((grad_part, grad_keys_part), 'head')  18.1 us
    dot_general x15, matrix products, product(): return jnp.einsum(form, former, latter, preferred_element_type=jnp.float32)  13.8 us
  transfers between devices with their start and end apart: 3, of which 3 were waited for; matrix products, arithmetic and copies ran while one was open for 2% of the time, Pallas kernels for 0%

commit v1 on v0

--- a/solution.py
+++ b/solution.py
@@ -3,6 +3,7 @@
 import jax.numpy as jnp
 from jax import lax
 from jax.sharding import PartitionSpec as P
+from jax.lax import all_to_all, axis_size
 
 C = 16
 PQ = 4
@@ -274,7 +275,13 @@
     scores = scores.reshape(2 * head_count, rows_n, local_k)
     scores = lax.all_to_all(scores, "row", split_axis=1, concat_axis=1, tiled=True)
     scores = jnp.transpose(scores, (1, 0, 2))
-    side_all = lax.all_gather(query_side, "row", axis=0, tiled=True)
+
+    def put_ratios_on_mesh(x_local):
+        placed = all_to_all(jnp.stack(axis_size("row") * [x_local], axis=0), "row", 0, 0)
+        met_up = jnp.concatenate(placed, 0)
+        return met_up
+
+    side_all = put_ratios_on_mesh(query_side)
     key_rows = key_terms(
         scores[:, :head_count],
         scores[:, head_count:],

time: 623 us -> 280 us (0.45)
  blocking collectives: 369 us -> 11 us
  waiting for transfers between devices: 135 us -> 146 us
  starting transfers between devices: 6.41 us -> 15.7 us
    all_gather x1 -> x0, blocking collectives: 304 us -> none  [shards(): side_all = lax.all_gather(query_side, 'row', axis=0, tiled=True)]
    psum x1, blocking collectives: 65.1 us -> 11 us  [shards(): output = lax.psum(output_part, 'head').astype(jnp.bfloat16)]
    all_to_all x0 -> x1, waiting for transfers between devices: none -> 9.41 us  [put_ratios_on_mesh(): all_to_all(jnp.stack(axis_size('row') * [x_local], axis=0), 'row', 0, 0)]
    all_to_all x0 -> x1, starting transfers between devices: none -> 9.23 us  [put_ratios_on_mesh(): all_to_all(jnp.stack(axis_size('row') * [x_local], axis=0), 'row', 0, 0)]
  transfers between devices with their start and end apart: 3 -> 4, of which waited for: 3 -> 4; matrix products, arithmetic and copies ran while one was open for 2% -> 4% of each run, Pallas kernels for 0% -> 0%
where the time goes in v1:
time: 280 us; the launch traced here: 279 us
  waiting for transfers between devices  146 us (52%)
  local copies, waits for them, and re-layouts  46.3 us (17%)
  matrix products  39.8 us (14%)
  starting transfers between devices  15.7 us (6%)
  between operations  14.8 us (5%)
  blocking collectives  11 us (4%)
  other arithmetic  5.24 us (2%)
    all_gather x1, waiting for transfers between devices, shards(): gathered = lax.all_gather(packed, 'row', axis=0, tiled=True)  108 us
    psum x1, waiting for transfers between devices, shards(): grad_query, grad_keys = lax.psum((grad_part, grad_keys_part), 'head')  18.1 us
    slice x7, local copies, waits for them, and re-layouts, split_columns(): lax.slice_in_dim(packed, cursor, cursor + extent, axis=axis_index)  15.7 us
    dot_general x15, matrix products, product(): return jnp.einsum(form, former, latter, preferred_element_type=jnp.float32)  13 us
    unnamed x74, local copies, waits for them, and re-layouts  11.9 us
    psum x1, blocking collectives, shards(): output = lax.psum(output_part, 'head').astype(jnp.bfloat16)  11 us
    all_to_all x1, waiting for transfers between devices, shards(): lax.all_to_all(scores, 'row', split_axis=1, concat_axis=1, tiled=True)  10.4 us
    dot_general x4, matrix products, rotate(): jnp.einsum('xyn,nhpy->nhpx', rotation, vectors, precision=lax.Precision.H...  10.4 us
  transfers between devices with their start and end apart: 4, of which 4 were waited for; matrix products, arithmetic and copies ran while one was open for 4% of the time, Pallas kernels for 0%

profile of v1, /device:TPU:1, one launch (start us, length us, event | category | flops | bytes accessed | tf_op | source)
XLA Modules:
  0.0 278.9 jit_solution(2840662058819157597)
XLA Ops:
  7.2 0.8 slice_bitcast_fusion
  8.1 0.7 reshape.330
  8.9 0.9 fusion.64
  10.2 7.5 %fusion.65 = f32[64,3,4,3]{2,3,1,0:T(4,128)S(1)} fusion(f32[64,3,4,3]{3,2,1,0:T(4,128)S(1)} %copy.144, f32[3,3,64,1]{0,1,3,2:T(4,128)S(1)} %copy.203), kind=kOutput, calls=%fused_computation.113 | convolution fusion | flops 82944 | bytes 20736 | tf_op jit(solution)/shard_map/xyn,nhpy->nhpx/dot_general | solution.py:28
  18.4 1.1 fusion.7
  19.7 0.9 convolution_convert_fusion.3
  20.6 0.9 convolution_convert_fusion.4
  21.5 0.7 copy.153
  22.7 0.8 reshape.339
  23.5 0.3 fusion.52
  23.8 0.4 multiply_reduce_fusion.2
  24.4 0.7 reshape_reshape.13
  25.1 0.6 copy.171
  25.7 0.6 reshape.342
  26.4 0.9 fusion.18
  27.4 0.6 sub.56
  28.0 0.7 reshape.340
  28.8 0.7 copy.162
  29.5 0.6 fusion.62
  30.0 0.6 reshape.355
  30.6 0.6 broadcast_multiply_fusion
  31.2 108.1 %all-gather.2.cloned.1.call-done = bf16[8192,204]{1,0:T(8,128)(2,1)} async-done(((bf16[64,204]{1,0:T(8,128)(2,1)}), bf16[8192,204]{1,0:T(8,128)(2,1)}) %all-gather.2.cloned.1.call-update) | async-done | bytes 3342352 | tf_op jit(solution)/shard_map/all_gather | solution.py:246
  139.3 4.2 %slice.77 = bf16[8192,36]{1,0:T(8,128)(2,1)} slice(bf16[8192,204]{1,0:T(8,128)(2,1)} %all-gather.2.cloned.1.call-done), slice={[0:8192], [96:132]} | slice | bytes 1179648 | tf_op jit(solution)/shard_map/slice | solution.py:39
  143.6 2.9 %copy.156 = bf16[8192,36]{0,1:T(8,128)(2,1)} copy(bf16[8192,36]{1,0:T(8,128)(2,1)} %slice.77) | data formatting | bytes 1179648 | tf_op jit(solution)/shard_map/slice | solution.py:39
  146.5 1.2 reshape.341
  147.7 1.0 multiply_reduce_fusion
  149.0 4.9 %fusion.59 = (bf16[8192,48]{1,0:T(8,128)(2,1)}, bf16[8192,48]{1,0:T(8,128)(2,1)}) fusion(bf16[8192,204]{1,0:T(8,128)(2,1)} %all-gather.2.cloned.1.call-done), kind=kLoop, calls=%fused_computation.106 | loop fusion | bytes 3145728 | tf_op jit(solution)/shard_map/slice | solution.py:39
  153.9 2.7 copy.216
  156.6 1.4 fusion.67
  158.0 1.7 fusion.63
  159.9 0.7 fusion.57
  160.7 3.6 %slice.78 = bf16[8192,72]{1,0:T(8,128)(2,1)} slice(bf16[8192,204]{1,0:T(8,128)(2,1)} %all-gather.2.cloned.1.call-done), slice={[0:8192], [132:204]} | slice | bytes 2359296 | tf_op jit(solution)/shard_map/slice | solution.py:39
  164.2 3.8 %copy.217 = bf16[8192,72]{0,1:T(8,128)(2,1)} copy(bf16[8192,72]{1,0:T(8,128)(2,1)} %slice.78) | data formatting | bytes 2359296
  168.0 1.7 fusion.29
  169.7 0.7 bitcast_subtract_fusion.1
  170.4 0.7 sub.59
  171.1 1.6 fusion.61
  172.7 0.7 fusion.41
  173.4 1.5 convolution_convert_fusion.6
  174.9 1.4 copy.163
  176.3 1.3 reshape.409
  177.6 1.3 reshape_reshape.14
  178.9 2.2 fusion.70
  181.1 2.6 copy.215
  183.8 1.4 fusion.50
  185.2 1.8 fusion.20
  187.0 0.8 convert_reduce_fusion
  187.8 1.0 fusion.25
  188.8 0.4 fusion.27
  189.2 0.4 fusion.31
  189.7 0.4 fusion.15
  190.4 0.9 reshape.425
  191.4 0.7 stack.2
  192.1 9.2 %all-to-all-start = ((bf16[128,1,204]{2,1,0:T(2,128)(2,1)}), bf16[128,1,204]{2,1,0:T(2,128)(2,1)S(1)}, u32[]{:S(2)}, u32[]{:S(2)}) async-start(bf16[128,1,204]{2,1,0:T(2,128)(2,1)} %stack.2), calls=%async_computation | async-start | bytes 262144 | tf_op jit(solution)/shard_map/all_to_all | solution.py:280
  202.9 9.4 %all-to-all-done = bf16[128,1,204]{2,1,0:T(2,128)(2,1)S(1)} async-done(((bf16[128,1,204]{2,1,0:T(2,128)(2,1)}), bf16[128,1,204]{2,1,0:T(2,128)(2,1)S(1)}, u32[]{:S(2)}, u32[]{:S(2)}) %all-to-all-start) | async-done | bytes 52256 | tf_op jit(solution)/shard_map/all_to_all | solution.py:280
  212.3 6.1 %all-to-all-start.1 = ((bf16[128,2,192]{2,1,0:T(2,128)(2,1)}), bf16[128,2,192]{2,1,0:T(2,128)(2,1)S(1)}, u32[]{:S(2)}, u32[]{:S(2)}) async-start(bf16[128,2,192]{2,1,0:T(2,128)(2,1)} %reshape.425), calls=%async_computation.1 | async-start | bytes 262144 | tf_op jit(solution)/shard_map/all_to_all | solution.py:276
  218.5 0.3 all-reduce.3.cloned.1.call-start
  219.0 10.4 %all-to-all-done.1 = bf16[128,2,192]{2,1,0:T(2,128)(2,1)S(1)} async-done(((bf16[128,2,192]{2,1,0:T(2,128)(2,1)}), bf16[128,2,192]{2,1,0:T(2,128)(2,1)S(1)}, u32[]{:S(2)}, u32[]{:S(2)}) %all-to-all-start.1) | async-done | bytes 98336 | tf_op jit(solution)/shard_map/all_to_all | solution.py:276
  230.3 1.0 convolution_convert_fusion
  231.9 7.4 %convolution_convert_fusion.1 = bf16[64,3,4,3]{2,3,1,0:T(4,128)(2,1)S(1)} fusion(f32[64,3,4,3]{3,2,1,0:T(4,128)S(1)} %copy.174, f32[3,3,64,1]{0,1,3,2:T(4,128)S(1)} %copy.203), kind=kOutput, calls=%fused_computation.12 | convolution fusion | flops 85248 | bytes 16128 | tf_op jit(solution)/shard_map/xyn,nhpx->nhpy/dot_general | solution.py:32
  240.5 0.8 convolution_add_fusion.2
  241.5 11.0 %all-reduce = (bf16[1,384]{1,0:T(2,128)(2,1)}, f32[1,384]{1,0:T(1,128)}) all-reduce(f32[1,384]{1,0:T(1,128)S(1)} %fusion.69, f32[1,384]{1,0:T(1,128)S(1)} %add.116), channel_id=1, replica_groups=mesh['row'=128,'head'=2] {'head'}, use_global_device_ids=true, to_apply=%region_5.6 | all-reduce | flops 768 | bytes 5376 | tf_op jit(solution)/shard_map/psum | solution.py:270
  252.5 18.1 %all-reduce.3.cloned.1.call-done = f32[64,384]{1,0:T(8,128)} async-done(((f32[64,384]{1,0:T(8,128)}), f32[64,384]{1,0:T(8,128)}) %all-reduce.3.cloned.1.call-update) | async-done | bytes 98320 | tf_op jit(solution)/shard_map/psum | solution.py:296
  270.6 1.5 copy.247
  (145 shorter events, 7.7 us)
Async XLA Ops:
  7.2 150.8 %copy-start = (bf16[1,8192,128]{2,1,0:T(8,128)(2,1)S(1)}, bf16[1,8192,128]{2,1,0:T(8,128)(2,1)}, u32[]{:S(2)}) copy-start(bf16[1,8192,128]{2,1,0:T(8,128)(2,1)} %param.17) | copy-start | bytes 6291460
  7.2 10.8 %copy-start.4 = (bf16[64,384]{1,0:T(8,128)(2,1)S(1)}, bf16[64,384]{1,0:T(8,128)(2,1)}, u32[]{:S(2)}) copy-start(bf16[64,384]{1,0:T(8,128)(2,1)} %param.16) | copy-start | bytes 147460
  7.2 10.8 %copy-start.6 = (bf16[384,72]{0,1:T(8,128)(2,1)S(1)}, bf16[384,72]{0,1:T(8,128)(2,1)}, u32[]{:S(2)}) copy-start(bf16[384,72]{0,1:T(8,128)(2,1)} %param.25) | copy-start | bytes 165892
  7.2 132.1 %all-gather.2.cloned.1.call-start = ((), (), s32[]{:S(2)}) async-start(), calls=%async_computation.2 | async-start | bytes 4227072 | tf_op jit(solution)/shard_map/all_gather | solution.py:246
  8.8 13.5 %copy-start.3 = (bf16[528,384]{1,0:T(8,128)(2,1)S(1)}, bf16[528,384]{1,0:T(8,128)(2,1)}, u32[]{:S(2)}) copy-start(bf16[528,384]{1,0:T(8,128)(2,1)} %param.28) | copy-start | bytes 1216516
  8.8 13.5 %copy-start.27 = (bf16[1,384]{1,0:T(2,128)(2,1)S(1)}, bf16[1,384]{1,0:T(2,128)(2,1)}, u32[]{:S(2)}) copy-start(bf16[1,384]{1,0:T(2,128)(2,1)} %param.29) | copy-start | bytes 2308
  9.9 12.7 %copy-start.32 = (f32[12,1]{0,1:T(1,128)S(1)}, f32[12,1]{0,1:T(1,128)}, u32[]{:S(2)}) copy-start(f32[12,1]{0,1:T(1,128)} %param.18) | copy-start | bytes 148
  10.1 13.4 %copy-start.31 = (bf16[1,384]{1,0:T(2,128)(2,1)S(1)}, bf16[1,384]{1,0:T(2,128)(2,1)}, u32[]{:S(2)}) copy-start(bf16[1,384]{1,0:T(2,128)(2,1)} %param.15) | copy-start | bytes 2308
  10.1 20.5 %copy-start.33 = (f32[3]{0:T(128)S(1)}, f32[3]{0:T(128)}, u32[]{:S(2)}) copy-start(f32[3]{0:T(128)} %param.26) | copy-start | bytes 40
  22.5 121.0 %copy-start.15 = (f32[1,3,176]{2,1,0:T(4,128)}, f32[1,3,176]{2,1,0:T(4,128)S(1)}, u32[]{:S(2)}) copy-start(f32[1,3,176]{2,1,0:T(4,128)S(1)} %copy.194) | copy-start | bytes 6340
  22.6 121.0 %copy-start.17 = (bf16[1,3,176]{2,1,0:T(4,128)(2,1)}, bf16[1,3,176]{2,1,0:T(4,128)(2,1)S(1)}, u32[]{:S(2)}) copy-start(bf16[1,3,176]{2,1,0:T(4,128)(2,1)S(1)} %copy.242) | copy-start | bytes 3172
  22.7 4.6 %copy-start.18 = (f32[3,3,1]{1,0,2:T(4,128)}, f32[3,3,1]{1,0,2:T(4,128)S(1)}, u32[]{:S(2)}) copy-start(f32[3,3,1]{1,0,2:T(4,128)S(1)} %reshape.373) | copy-start | bytes 112
  27.3 116.3 %copy-start.24 = (bf16[48]{0:T(256)(128)(2,1)}, bf16[48]{0:T(256)(128)(2,1)S(1)}, u32[]{:S(2)}) copy-start(bf16[48]{0:T(256)(128)(2,1)S(1)} %fusion.18) | copy-start | bytes 292
  153.9 4.1 %copy-start.29 = (bf16[3,128]{1,0:T(4,128)(2,1)S(1)}, bf16[3,128]{1,0:T(4,128)(2,1)}, u32[]{:S(2)}) copy-start(bf16[3,128]{1,0:T(4,128)(2,1)} %param.27) | copy-start | bytes 2308
  183.8 4.0 %copy-start.5 = (bf16[1,3,8192]{2,1,0:T(4,128)(2,1)S(1)}, bf16[1,3,8192]{2,1,0:T(4,128)(2,1)}, u32[]{:S(2)}) copy-start(bf16[1,3,8192]{2,1,0:T(4,128)(2,1)} %get-tuple-element.9) | copy-start | bytes 147460
  185.2 3.6 %copy-start.1 = (bf16[8192,48]{0,1:T(8,128)(2,1)S(1)}, bf16[8192,48]{0,1:T(8,128)(2,1)}, u32[]{:S(2)}) copy-start(bf16[8192,48]{0,1:T(8,128)(2,1)} %copy.216) | copy-start | bytes 2359300
  187.0 2.2 copy-start.2
  189.2 2.1 copy-start.23
  189.2 2.1 copy-start.25
  189.2 2.1 copy-start.26
  189.2 2.1 copy-start.30
  189.6 11.8 %copy-start.19 = (bf16[3,12]{1,0:T(4,128)(2,1)S(1)}, bf16[3,12]{1,0:T(4,128)(2,1)}, u32[]{:S(2)}) copy-start(bf16[3,12]{1,0:T(4,128)(2,1)} %reshape.342) | copy-start | bytes 220
  189.6 11.8 %copy-start.20 = (f32[3]{0:T(128)S(1)}, f32[3]{0:T(128)}, u32[]{:S(2)}) copy-start(f32[3]{0:T(128)} %get-tuple-element.5) | copy-start | bytes 40
  189.6 11.8 %copy-start.22 = (f32[3]{0:T(128)S(1)}, f32[3]{0:T(128)}, u32[]{:S(2)}) copy-start(f32[3]{0:T(128)} %get-tuple-element.7) | copy-start | bytes 40
  189.6 11.8 %copy-start.28 = (f32[3,1,12]{2,1,0:T(1,128)S(1)}, f32[3,1,12]{2,1,0:T(1,128)}, u32[]{:S(2)}) copy-start(f32[3,1,12]{2,1,0:T(1,128)} %fusion.25) | copy-start | bytes 436
  189.6 11.9 %copy-start.14 = (f32[3,3]{1,0:T(4,128)S(1)}, f32[3,3]{1,0:T(4,128)}, u32[]{:S(2)}) copy-start(f32[3,3]{1,0:T(4,128)} %reshape.340) | copy-start | bytes 112
  189.6 12.6 %copy-start.16 = (bf16[3,8,3]{1,2,0:T(4,128)(2,1)S(1)}, bf16[3,8,3]{1,2,0:T(4,128)(2,1)}, u32[]{:S(2)}) copy-start(bf16[3,8,3]{1,2,0:T(4,128)(2,1)} %get-tuple-element.15) | copy-start | bytes 436
  189.7 13.1 %copy-start.13 = (bf16[384,48]{0,1:T(8,128)(2,1)S(1)}, bf16[384,48]{0,1:T(8,128)(2,1)}, u32[]{:S(2)}) copy-start(bf16[384,48]{0,1:T(8,128)(2,1)} %param.20) | copy-start | bytes 110596
  190.4 41.1 %copy-start.12 = (f32[64,3,4,3]{0,1,3,2:T(4,128)S(1)}, f32[64,3,4,3]{0,1,3,2:T(4,128)}, u32[]{:S(2)}) copy-start(f32[64,3,4,3]{0,1,3,2:T(4,128)} %copy.171) | copy-start | bytes 27652
  190.4 41.1 %copy-start.21 = (f32[3]{0:T(128)S(1)}, f32[3]{0:T(128)}, u32[]{:S(2)}) copy-start(f32[3]{0:T(128)} %get-tuple-element.5) | copy-start | bytes 40
  192.1 20.2 %all-to-all-start = ((bf16[128,1,204]{2,1,0:T(2,128)(2,1)}), bf16[128,1,204]{2,1,0:T(2,128)(2,1)S(1)}, u32[]{:S(2)}, u32[]{:S(2)}) async-start(bf16[128,1,204]{2,1,0:T(2,128)(2,1)} %stack.2), calls=%async_computation | async-start | bytes 262144 | tf_op jit(solution)/shard_map/all_to_all | solution.py:280
  212.3 17.1 %all-to-all-start.1 = ((bf16[128,2,192]{2,1,0:T(2,128)(2,1)}), bf16[128,2,192]{2,1,0:T(2,128)(2,1)S(1)}, u32[]{:S(2)}, u32[]{:S(2)}) async-start(bf16[128,2,192]{2,1,0:T(2,128)(2,1)} %reshape.425), calls=%async_computation.1 | async-start | bytes 262144 | tf_op jit(solution)/shard_map/all_to_all | solution.py:276
  218.5 52.1 %all-reduce.3.cloned.1.call-start = ((), (), s32[]{:S(2)}) async-start(), calls=%async_computation.3 | async-start | bytes 196608 | tf_op jit(solution)/shard_map/psum | solution.py:296
  218.9 21.0 %copy-start.8 = (bf16[384,48]{0,1:T(8,128)(2,1)S(1)}, bf16[384,48]{0,1:T(8,128)(2,1)}, u32[]{:S(2)}) copy-start(bf16[384,48]{0,1:T(8,128)(2,1)} %param.21) | copy-start | bytes 110596
  218.9 21.1 %copy-start.9 = (bf16[384,48]{0,1:T(8,128)(2,1)S(1)}, bf16[384,48]{0,1:T(8,128)(2,1)}, u32[]{:S(2)}) copy-start(bf16[384,48]{0,1:T(8,128)(2,1)} %param.22) | copy-start | bytes 110596
  229.6 10.7 %copy-start.11 = (bf16[384,36]{0,1:T(8,128)(2,1)S(1)}, bf16[384,36]{0,1:T(8,128)(2,1)}, u32[]{:S(2)}) copy-start(bf16[384,36]{0,1:T(8,128)(2,1)} %param.24) | copy-start | bytes 82948
  229.6 10.9 %copy-start.7 = (bf16[384,72]{0,1:T(8,128)(2,1)S(1)}, bf16[384,72]{0,1:T(8,128)(2,1)}, u32[]{:S(2)}) copy-start(bf16[384,72]{0,1:T(8,128)(2,1)} %param.25) | copy-start | bytes 165892
  230.0 11.3 %copy-start.10 = (bf16[384,36]{0,1:T(8,128)(2,1)S(1)}, bf16[384,36]{0,1:T(8,128)(2,1)}, u32[]{:S(2)}) copy-start(bf16[384,36]{0,1:T(8,128)(2,1)} %param.23) | copy-start | bytes 82948
Sparse Core Ops, SparseCore 0:
  22.4 116.8 all-gather.1
  241.4 29.0 all-reduce.2
